TPU v7x, 128 devices: a whole 4x4x4 slice. The times are simulated.
128 devices in a mesh: animal: 16 (over z, x_lo, core), snp: 8 (over x_hi, y).
Axes of the slice: x: 4 (x_hi: 2, x_lo: 2; x = x_hi * 2 + x_lo), y: 4, z: 4, core: 2. Of those that a mesh axis runs over, the one named last changes fastest.
Arguments:
- genotypes: int32 [32768, 8192], P('animal', 'snp'), may hold values from 0 to 2730, as said below
- allele_frequency: float32 [49152], P('snp'), may hold values from 0.05 to 0.5
- family_size: int32 [256], P('animal'), may hold values from 40 to 128, as said below
- rel_family: int32 [256], P('animal'), may hold values from 0 to 255, as said below
- rel_count: int32 [256], P('animal'), may hold values from 8 to 128, as said below
- own_block: bfloat16 [256, 128, 128], P('animal'), may hold values from -0.5 to 3
- rel_block: bfloat16 [256, 128, 128], P('animal'), may hold values from -0.5 to 0.5
- prior_solution: bfloat16 [32768, 128], P('animal'), may hold values from -6 to 6
- right_side: float32 [32768, 128], P('animal'), may hold values from -6 to 6
- step_scale: float32 [32768], P('animal'), may hold values from 0.1 to 0.3
Outputs:
- solution: float32 [32768, 128], P(('animal', 'snp'))
- residual: float32 [32768, 128], P(('animal', 'snp'))
Inputs may be any that keep to these rules, and one draw needn't show every extreme that they name: `genotypes`: bits 2k and 2k + 1 of word w of a row hold the code 0, 1 or 2 of marker 6w + k, for k = 0 to 5; higher bits are zero; some word has all six codes 0 and some word all six codes 2. `family_size`: some family has all 128 slots live. `rel_family`: family f's relative family lies in the same block of 16 consecutive families as f or in one of the 3 blocks before it, and in the block exactly 3 before it for some family of every block that has one. `rel_count`: some family takes all 128 rows.
All inputs are finite; a program needn't handle non-finite values.
Results may differ from a plain program's by a relative error of at most 0.007.
Values may be sent and summed in bfloat16 or wider, within the bound.
A program may use at most 192 MiB of HBM per device.

v0:
```python
import jax
import jax.numpy as jnp
from jax import lax
from jax.sharding import PartitionSpec as P

SNPS = 49152
ITERS = 2
RSPAN = 3
GEN_WEIGHT = 6.0


def shifted(array, axis, by):
    count = lax.axis_size(axis)
    pairs = [(i, i + by) for i in range(count) if 0 <= i + by < count]
    return lax.ppermute(array, axis, pairs)


def in_blocks(array, dim, count):
    before, after = (array.shape[:dim], array.shape[dim + 1 :])
    return jnp.moveaxis(array.reshape(*before, count, -1, *after), dim, 0)


def sum_at_owner(array, axis, dim):
    tiles = in_blocks(array, dim, lax.axis_size(axis))
    arrived = lax.all_to_all(tiles, axis, split_axis=0, concat_axis=0, tiled=True)
    return arrived.sum(axis=0)


def copy_for_each(array, axis):
    copies = jnp.broadcast_to(array, (lax.axis_size(axis), *array.shape))
    return lax.all_to_all(copies, axis, split_axis=0, concat_axis=0, tiled=True)


def joined_along(tiles, dim):
    lengths = list(tiles.shape[1:])
    lengths[dim] *= tiles.shape[0]
    return jnp.moveaxis(tiles, 0, dim).reshape(lengths)


def gathered_copies(array, axis, dim):
    tiles = copy_for_each(array, axis)
    return joined_along(tiles, dim)


def decode_rows(genotypes, allele_frequency, live_rows):
    bit_shifts = 2 * jnp.arange(6, dtype=jnp.int32)
    dosage_states = jnp.bitwise_and(
        jnp.right_shift(genotypes[:, :, None], bit_shifts[None, None, :]), 3
    )
    dosage_states = dosage_states.reshape(genotypes.shape[0], genotypes.shape[1] * 6).astype(
        jnp.float32
    )
    centered = (dosage_states - 2.0 * allele_frequency[None, :]) * live_rows[:, None]
    return centered.astype(jnp.bfloat16)


def decode_blocks(genotypes, allele_frequency, live_rows, family_count, block_order):
    group_count = family_count // 4
    group_rows = 4 * block_order
    packed_marker_groups = genotypes.reshape(group_count, group_rows, genotypes.shape[1])
    live_groups = live_rows.reshape(group_count, group_rows)

    def decode_group(inputs):
        return decode_rows(inputs[0], allele_frequency, inputs[1])

    decoded = lax.map(decode_group, (packed_marker_groups, live_groups))
    return decoded.reshape(family_count * block_order, genotypes.shape[1] * 6)


def live_mask(family_size, block_order):
    slot_index = jnp.arange(block_order, dtype=jnp.int32)
    return (slot_index[None, :] < family_size[:, None]).astype(jnp.float32).reshape(-1)


def mask_rows(relatives, rel_count, block_order):
    keep_rows = jnp.arange(block_order, dtype=jnp.int32)[None, :, None] < rel_count[:, None, None]
    return jnp.where(keep_rows, relatives, jnp.zeros_like(relatives))


def fetch_relatives(solution_half, rel_family, rel_count, family_count, block_order, columns):
    lower_blocks = [solution_half]
    for starting_displacement in range(1, RSPAN + 1):
        lower_blocks.append(shifted(solution_half, "animal", starting_displacement))
    stacked = jnp.stack(lower_blocks).reshape((RSPAN + 1) * family_count, block_order, columns)
    own_device = lax.axis_index("animal")
    distance = own_device - rel_family // family_count
    position = distance * family_count + rel_family % family_count
    relatives = jnp.take(stacked, position, axis=0)
    return mask_rows(relatives, rel_count, block_order)


def pedigree_term(own_block, rel_block, own_half, relatives):
    first_part = jnp.einsum("fij,fjk->fik", own_block, own_half, preferred_element_type=jnp.float32)
    return first_part + jnp.einsum(
        "fij,fjk->fik", rel_block, relatives, preferred_element_type=jnp.float32
    )


def per_device(
    genotypes,
    allele_frequency,
    family_size,
    rel_family,
    rel_count,
    own_block,
    rel_block,
    prior_solution,
    right_side,
    step_scale,
):
    family_count = own_block.shape[0]
    block_order = own_block.shape[1]
    columns = prior_solution.shape[1]
    row_count = family_count * block_order
    live_rows = live_mask(family_size, block_order)
    centered = decode_blocks(genotypes, allele_frequency, live_rows, family_count, block_order)
    share_families = family_count // lax.axis_size("snp")
    share_rows = share_families * block_order
    share_position = lax.axis_index("snp")
    family_first = share_position * share_families
    row_first = share_position * share_rows
    relative_part = lax.dynamic_slice_in_dim(rel_family, family_first, share_families, 0)
    count_part = lax.dynamic_slice_in_dim(rel_count, family_first, share_families, 0)
    solution_now = live_rows[:, None] * prior_solution.astype(jnp.float32)
    residual = jnp.zeros((row_count, columns), jnp.float32)
    for iteration in range(ITERS):
        solution_half = solution_now.astype(jnp.bfloat16)
        partial_sum = lax.dot_general(
            centered, solution_half, (((0,), (0,)), ((), ())), preferred_element_type=jnp.float32
        )
        snp_half = lax.psum(partial_sum, "animal").astype(jnp.bfloat16)
        genomic_part = jnp.dot(centered, snp_half, preferred_element_type=jnp.float32)
        relatives = fetch_relatives(
            solution_half, relative_part, count_part, family_count, block_order, columns
        )
        genomic = sum_at_owner(genomic_part, "snp", 0)
        own_part = lax.dynamic_slice_in_dim(own_block, family_first, share_families, 0)
        couple_part = lax.dynamic_slice_in_dim(rel_block, family_first, share_families, 0)
        own_half = lax.dynamic_slice_in_dim(solution_half, row_first, share_rows, 0).reshape(
            share_families, block_order, columns
        )
        pedigree = pedigree_term(own_part, couple_part, own_half, relatives).reshape(
            share_rows, columns
        )
        live_part = lax.dynamic_slice_in_dim(live_rows, row_first, share_rows, 0)
        right_part = lax.dynamic_slice_in_dim(right_side, row_first, share_rows, 0)
        scale_part = lax.dynamic_slice_in_dim(step_scale, row_first, share_rows, 0)
        solution_part = lax.dynamic_slice_in_dim(solution_now, row_first, share_rows, 0)
        residual = live_part[:, None] * (
            right_part - solution_part - GEN_WEIGHT / SNPS * genomic - pedigree
        )
        solution_part = solution_part + scale_part[:, None] * residual
        if iteration + 1 < ITERS:
            solution_now = gathered_copies(solution_part.astype(jnp.bfloat16), "snp", 0).astype(
                solution_part.dtype
            )
        else:
            solution_now = solution_part
    return (solution_now, residual)


def solution(mesh):
    in_specs = (
        P("animal", "snp"),
        P("snp"),
        P("animal"),
        P("animal"),
        P("animal"),
        P("animal", None, None),
        P("animal", None, None),
        P("animal", None),
        P("animal", None),
        P("animal"),
    )
    out_specs = (P(("animal", "snp"), None), P(("animal", "snp"), None))
    return jax.shard_map(
        per_device, mesh=mesh, in_specs=in_specs, out_specs=out_specs, check_vma=False
    )
```

profile of v0, /device:TPU:0, one launch (start us, length us, event | category | flops | bytes accessed | tf_op | source)
XLA Modules:
  0.0 511.2 jit_solution(6328784146243284202)
XLA Ops:
  16.3 210.8 %while.10 = (s32[]{:T(128)}, bf16[4,512,6144]{2,1,0:T(8,128)(2,1)}, s32[4,512,1024]{2,1,0:T(8,128)}, f32[6144]{0:T(1024)}, f32[4,512]{1,0:T(4,128)S(1)}, /*index=5*/s32[]{:T(128)}) while((s32[]{:T(128)}, bf16[4,512,6144]{2,1,0:T(8,128)(2,1)}, s32[4,512,1024]{2,1,0:T(8,128)}, f32[6144]{0:T(1024)}, f32[4,512]{1,0:T(4,128)S(1)}, ...), condition=%wide.region_1.2_spmd, body=%wide.region_0.1_spmd.sunk | while | flops 18880520 | bytes 92551832 | solution.py:66
  21.4 8.0 %shift_right_arithmetic.39 = s32[512,1024,6]{0,2,1:T(8,128)} broadcast(s32[512,1024]{0,1:T(8,128)S(1)} %bitcast.61), dimensions={0,1} | broadcast | bytes 14680064 | tf_op jit(solution)/shard_map/while/body/eval_jaxpr/shift_right_arithmetic | solution.py:48
  29.5 15.6 %shift_right_arithmetic.40 = s32[1,512,6144]{1,2,0:T(8,128)} reshape(s32[512,1024,6]{0,2,1:T(8,128)} %shift_right_arithmetic.39) | data formatting | bytes 25165824 | tf_op jit(solution)/shard_map/while/body/eval_jaxpr/shift_right_arithmetic | solution.py:48
  45.5 8.7 %multiply_convert_fusion.2 = bf16[1,512,6144]{1,2,0:T(8,128)(2,1)} fusion(s32[1,512,6144]{1,2,0:T(8,128)} %shift_right_arithmetic.40, f32[512]{0:T(512)S(1)} %bitcast.76, f32[6144]{0:T(1024)S(1)} %broadcast_multiply_fusion.2, s32[6144]{0:T(1024)S(1)} %shift_right_arithmetic.42), kind=kLoop, calls=%fused_computation.2.clone.1 | loop fusion | flops 18874368 | bytes 18925568 | tf_op jit(solution)/shard_map/while/body/eval_jaxpr/convert_element_type | solution.py:54
  54.2 8.7 %copy.25 = bf16[1,512,6144]{2,1,0:T(8,128)(2,1)} copy(bf16[1,512,6144]{1,2,0:T(8,128)(2,1)} %multiply_convert_fusion.2) | data formatting | bytes 12582912 | tf_op jit(solution)/shard_map/while/body/jit(dynamic_update_index_in_dim)/dynamic_update_slice | solution.py:66
  74.2 8.0 %shift_right_arithmetic.39 = s32[512,1024,6]{0,2,1:T(8,128)} broadcast(s32[512,1024]{0,1:T(8,128)S(1)} %bitcast.61), dimensions={0,1} | broadcast | bytes 14680064 | tf_op jit(solution)/shard_map/while/body/eval_jaxpr/shift_right_arithmetic | solution.py:48
  82.2 15.6 %shift_right_arithmetic.40 = s32[1,512,6144]{1,2,0:T(8,128)} reshape(s32[512,1024,6]{0,2,1:T(8,128)} %shift_right_arithmetic.39) | data formatting | bytes 25165824 | tf_op jit(solution)/shard_map/while/body/eval_jaxpr/shift_right_arithmetic | solution.py:48
  98.2 8.7 %multiply_convert_fusion.2 = bf16[1,512,6144]{1,2,0:T(8,128)(2,1)} fusion(s32[1,512,6144]{1,2,0:T(8,128)} %shift_right_arithmetic.40, f32[512]{0:T(512)S(1)} %bitcast.76, f32[6144]{0:T(1024)S(1)} %broadcast_multiply_fusion.2, s32[6144]{0:T(1024)S(1)} %shift_right_arithmetic.42), kind=kLoop, calls=%fused_computation.2.clone.1 | loop fusion | flops 18874368 | bytes 18925568 | tf_op jit(solution)/shard_map/while/body/eval_jaxpr/convert_element_type | solution.py:54
  106.9 8.7 %copy.25 = bf16[1,512,6144]{2,1,0:T(8,128)(2,1)} copy(bf16[1,512,6144]{1,2,0:T(8,128)(2,1)} %multiply_convert_fusion.2) | data formatting | bytes 12582912 | tf_op jit(solution)/shard_map/while/body/jit(dynamic_update_index_in_dim)/dynamic_update_slice | solution.py:66
  134.9 15.6 %shift_right_arithmetic.40 = s32[1,512,6144]{1,2,0:T(8,128)} reshape(s32[512,1024,6]{0,2,1:T(8,128)} %shift_right_arithmetic.39) | data formatting | bytes 25165824 | tf_op jit(solution)/shard_map/while/body/eval_jaxpr/shift_right_arithmetic | solution.py:48
  150.9 8.7 %multiply_convert_fusion.2 = bf16[1,512,6144]{1,2,0:T(8,128)(2,1)} fusion(s32[1,512,6144]{1,2,0:T(8,128)} %shift_right_arithmetic.40, f32[512]{0:T(512)S(1)} %bitcast.76, f32[6144]{0:T(1024)S(1)} %broadcast_multiply_fusion.2, s32[6144]{0:T(1024)S(1)} %shift_right_arithmetic.42), kind=kLoop, calls=%fused_computation.2.clone.1 | loop fusion | flops 18874368 | bytes 18925568 | tf_op jit(solution)/shard_map/while/body/eval_jaxpr/convert_element_type | solution.py:54
  159.6 8.7 %copy.25 = bf16[1,512,6144]{2,1,0:T(8,128)(2,1)} copy(bf16[1,512,6144]{1,2,0:T(8,128)(2,1)} %multiply_convert_fusion.2) | data formatting | bytes 12582912 | tf_op jit(solution)/shard_map/while/body/jit(dynamic_update_index_in_dim)/dynamic_update_slice | solution.py:66
  179.6 8.0 %shift_right_arithmetic.39 = s32[512,1024,6]{0,2,1:T(8,128)} broadcast(s32[512,1024]{0,1:T(8,128)S(1)} %bitcast.61), dimensions={0,1} | broadcast | bytes 14680064 | tf_op jit(solution)/shard_map/while/body/eval_jaxpr/shift_right_arithmetic | solution.py:48
  187.6 15.6 %shift_right_arithmetic.40 = s32[1,512,6144]{1,2,0:T(8,128)} reshape(s32[512,1024,6]{0,2,1:T(8,128)} %shift_right_arithmetic.39) | data formatting | bytes 25165824 | tf_op jit(solution)/shard_map/while/body/eval_jaxpr/shift_right_arithmetic | solution.py:48
  203.6 8.7 %multiply_convert_fusion.2 = bf16[1,512,6144]{1,2,0:T(8,128)(2,1)} fusion(s32[1,512,6144]{1,2,0:T(8,128)} %shift_right_arithmetic.40, f32[512]{0:T(512)S(1)} %bitcast.76, f32[6144]{0:T(1024)S(1)} %broadcast_multiply_fusion.2, s32[6144]{0:T(1024)S(1)} %shift_right_arithmetic.42), kind=kLoop, calls=%fused_computation.2.clone.1 | loop fusion | flops 18874368 | bytes 18925568 | tf_op jit(solution)/shard_map/while/body/eval_jaxpr/convert_element_type | solution.py:54
  212.3 8.7 %copy.25 = bf16[1,512,6144]{2,1,0:T(8,128)(2,1)} copy(bf16[1,512,6144]{1,2,0:T(8,128)(2,1)} %multiply_convert_fusion.2) | data formatting | bytes 12582912 | tf_op jit(solution)/shard_map/while/body/jit(dynamic_update_index_in_dim)/dynamic_update_slice | solution.py:66
  227.1 12.9 %fusion.39 = f32[6144,128]{1,0:T(8,128)} fusion(bf16[2048,6144]{1,0:T(8,128)(2,1)} %bitcast.77, bf16[2048,128]{1,0:T(8,128)(2,1)} %get-tuple-element.51), kind=kOutput, calls=%fused_computation.72 | convolution fusion | flops 3221225472 | bytes 28835840 | tf_op jit(solution)/shard_map/dot_general | solution.py:128
  240.0 78.8 %all-reduce.2 = bf16[6144,128]{1,0:T(8,128)(2,1)S(1)} all-reduce(f32[6144,128]{1,0:T(8,128)} %fusion.39), channel_id=1, replica_groups=mesh['animal'=16,'snp'=8] {'animal'}, use_global_device_ids=true, to_apply=%region_2.3 | all-reduce | flops 786432 | bytes 4718592 | tf_op jit(solution)/shard_map/psum | solution.py:131
  318.8 12.6 %fusion.2 = f32[8,256,128]{2,1,0:T(8,128)} fusion(bf16[8,256,6144]{2,1,0:T(8,128)(2,1)} %bitcast.78, bf16[6144,128]{1,0:T(8,128)(2,1)S(1)} %all-reduce.2), kind=kOutput, calls=%fused_computation.12 | convolution fusion | flops 3221225472 | bytes 27787264 | tf_op jit(solution)/shard_map/dot_general | solution.py:132
  353.4 14.6 %all_to_all.15 = bf16[8,256,128]{2,1,0:T(8,128)(2,1)S(1)} all-to-all(bf16[8,256,128]{2,1,0:T(8,128)(2,1)S(1)} %broadcast_in_dim.32), channel_id=1, replica_groups=mesh['animal'=16,'snp'=8] {'snp'}, dimensions={0} | all-to-all | bytes 1048576 | tf_op jit(solution)/shard_map/all_to_all | solution.py:31
  368.0 13.4 %fusion.40 = f32[6144,128]{1,0:T(8,128)} fusion(bf16[2048,6144]{1,0:T(8,128)(2,1)} %bitcast.79, bf16[2048,128]{1,0:T(8,128)(2,1)S(1)} %bitcast.63), kind=kOutput, calls=%fused_computation.73 | convolution fusion | flops 3221225472 | bytes 28835840 | tf_op jit(solution)/shard_map/dot_general | solution.py:128
  388.5 90.2 %all-reduce.3 = bf16[6144,128]{1,0:T(8,128)(2,1)} all-reduce(f32[6144,128]{1,0:T(8,128)} %fusion.40), channel_id=1, replica_groups=mesh['animal'=16,'snp'=8] {'animal'}, use_global_device_ids=true, to_apply=%region_4.6 | all-reduce | flops 786432 | bytes 4718592 | tf_op jit(solution)/shard_map/psum | solution.py:131
  478.7 12.9 %fusion = f32[8,256,128]{2,1,0:T(8,128)} fusion(bf16[8,256,6144]{2,1,0:T(8,128)(2,1)} %bitcast.80, bf16[6144,128]{1,0:T(8,128)(2,1)} %all-reduce.3), kind=kOutput, calls=%fused_computation.10 | convolution fusion | flops 3221225472 | bytes 27787264 | tf_op jit(solution)/shard_map/dot_general | solution.py:132
  501.2 8.3 %all-to-all-done.2 = f32[8,256,128]{2,1,0:T(8,128)S(1)} async-done(((f32[8,256,128]{2,1,0:T(8,128)}), f32[8,256,128]{2,1,0:T(8,128)S(1)}, u32[]{:S(2)}, u32[]{:S(2)}) %all-to-all-start.2) | async-done | bytes 1048608 | tf_op jit(solution)/shard_map/all_to_all | solution.py:25
  (92 shorter events, 110.8 us)
Async XLA Ops:
  0.6 340.3 %copy-start = (bf16[16,128,128]{2,1,0:T(8,128)(2,1)S(1)}, bf16[16,128,128]{2,1,0:T(8,128)(2,1)}, u32[]{:S(2)}) copy-start(bf16[16,128,128]{2,1,0:T(8,128)(2,1)} %param.19) | copy-start | bytes 1572868
  1.4 0.6 copy-start.2
  4.6 336.6 %collective-permute-start = (bf16[2048,128]{1,0:T(8,128)(2,1)}, bf16[2048,128]{1,0:T(8,128)(2,1)}, u32[]{:S(2)}, u32[]{:S(2)}) collective-permute-start(bf16[2048,128]{1,0:T(8,128)(2,1)} %get-tuple-element.51), channel_id=1, source_target_pairs={{0,8},{8,16},{16,24},{24,32},{32,40},{40,48},{48,56},{56,64},{64,7... | collective-permute-start | bytes 1572872 | tf_op jit(solution)/shard_map/ppermute | solution.py:15
  6.6 334.5 %collective-permute-start.1 = (bf16[2048,128]{1,0:T(8,128)(2,1)}, bf16[2048,128]{1,0:T(8,128)(2,1)}, u32[]{:S(2)}, u32[]{:S(2)}) collective-permute-start(bf16[2048,128]{1,0:T(8,128)(2,1)} %get-tuple-element.51), channel_id=1, source_target_pairs={{0,16},{8,24},{16,32},{24,40},{32,48},{40,56},{48,64},{56,72},{64,... | collective-permute-start | bytes 1572872 | tf_op jit(solution)/shard_map/ppermute | solution.py:15
  10.8 330.3 %collective-permute-start.2 = (bf16[2048,128]{1,0:T(8,128)(2,1)}, bf16[2048,128]{1,0:T(8,128)(2,1)}, u32[]{:S(2)}, u32[]{:S(2)}) collective-permute-start(bf16[2048,128]{1,0:T(8,128)(2,1)} %get-tuple-element.51), channel_id=1, source_target_pairs={{0,24},{8,32},{16,40},{24,48},{32,56},{40,64},{48,72},{56,80},{64,... | collective-permute-start | bytes 1572872 | tf_op jit(solution)/shard_map/ppermute | solution.py:15
  29.4 15.6 %copy-start.1 = (f32[6144]{0:T(1024)S(1)}, f32[6144]{0:T(1024)}, u32[]{:S(2)}) copy-start(f32[6144]{0:T(1024)} %get-tuple-element.98) | copy-start | bytes 73732 | tf_op jit(solution)/shard_map/while
  82.2 15.6 %copy-start.1 = (f32[6144]{0:T(1024)S(1)}, f32[6144]{0:T(1024)}, u32[]{:S(2)}) copy-start(f32[6144]{0:T(1024)} %get-tuple-element.98) | copy-start | bytes 73732 | tf_op jit(solution)/shard_map/while
  134.9 15.6 %copy-start.1 = (f32[6144]{0:T(1024)S(1)}, f32[6144]{0:T(1024)}, u32[]{:S(2)}) copy-start(f32[6144]{0:T(1024)} %get-tuple-element.98) | copy-start | bytes 73732 | tf_op jit(solution)/shard_map/while
  187.6 15.6 %copy-start.1 = (f32[6144]{0:T(1024)S(1)}, f32[6144]{0:T(1024)}, u32[]{:S(2)}) copy-start(f32[6144]{0:T(1024)} %get-tuple-element.98) | copy-start | bytes 73732 | tf_op jit(solution)/shard_map/while
  318.8 21.9 %copy-start.4 = (s32[16]{0:T(128)S(1)}, s32[16]{0:T(128)}, u32[]{:S(2)}) copy-start(s32[16]{0:T(128)} %param.18) | copy-start | bytes 196
  318.8 22.0 %copy-start.3 = (s32[16]{0:T(128)S(1)}, s32[16]{0:T(128)}, u32[]{:S(2)}) copy-start(s32[16]{0:T(128)} %param.17) | copy-start | bytes 196
  331.4 20.8 %all-to-all-start = ((f32[8,256,128]{2,1,0:T(8,128)}), f32[8,256,128]{2,1,0:T(8,128)S(1)}, u32[]{:S(2)}, u32[]{:S(2)}) async-start(f32[8,256,128]{2,1,0:T(8,128)} %fusion.2), calls=%async_computation | async-start | bytes 2097152 | tf_op jit(solution)/shard_map/all_to_all | solution.py:25
  381.4 113.9 %collective-permute-start.3 = (bf16[2048,128]{1,0:T(8,128)(2,1)S(1)}, bf16[2048,128]{1,0:T(8,128)(2,1)S(1)}, u32[]{:S(2)}, u32[]{:S(2)}) collective-permute-start(bf16[2048,128]{1,0:T(8,128)(2,1)S(1)} %bitcast.64), channel_id=1, source_target_pairs={{0,8},{8,16},{16,24},{24,32},{32,40},{40,48},{48,56},{56,64},{64,7... | collective-permute-start | bytes 1572872 | tf_op jit(solution)/shard_map/ppermute | solution.py:15
  382.7 112.6 %collective-permute-start.4 = (bf16[2048,128]{1,0:T(8,128)(2,1)S(1)}, bf16[2048,128]{1,0:T(8,128)(2,1)S(1)}, u32[]{:S(2)}, u32[]{:S(2)}) collective-permute-start(bf16[2048,128]{1,0:T(8,128)(2,1)S(1)} %bitcast.65), channel_id=1, source_target_pairs={{0,16},{8,24},{16,32},{24,40},{32,48},{40,56},{48,64},{56,72},{64,... | collective-permute-start | bytes 1572872 | tf_op jit(solution)/shard_map/ppermute | solution.py:15
  384.0 111.2 %collective-permute-start.5 = (bf16[2048,128]{1,0:T(8,128)(2,1)S(1)}, bf16[2048,128]{1,0:T(8,128)(2,1)}, u32[]{:S(2)}, u32[]{:S(2)}) collective-permute-start(bf16[2048,128]{1,0:T(8,128)(2,1)S(1)} %bitcast.66), channel_id=1, source_target_pairs={{0,24},{8,32},{16,40},{24,48},{32,56},{40,64},{48,72},{56,80},{64,... | collective-permute-start | bytes 1572872 | tf_op jit(solution)/shard_map/ppermute | solution.py:15
  491.5 17.9 %all-to-all-start.2 = ((f32[8,256,128]{2,1,0:T(8,128)}), f32[8,256,128]{2,1,0:T(8,128)S(1)}, u32[]{:S(2)}, u32[]{:S(2)}) async-start(f32[8,256,128]{2,1,0:T(8,128)} %fusion), calls=%async_computation.2 | async-start | bytes 2097152 | tf_op jit(solution)/shard_map/all_to_all | solution.py:25
where the time goes:
time: 515 us; the launch traced here: 511 us
  local copies, waits for them, and re-layouts  184 us (36%)
  blocking collectives  184 us (36%)
  matrix products  54.2 us (11%)
  other arithmetic  47 us (9%)
  starting transfers between devices  28.5 us (6%)
  waiting for transfers between devices  12.9 us (3%)
    psum x2, blocking collectives, per_device(): snp_half = lax.psum(partial_sum, 'animal').astype(jnp.bfloat16)  169 us
    shift_right_arithmetic x16, local copies, waits for them, and re-layouts, decode_rows(): jnp.right_shift(genotypes[:, :, None], bit_shifts[None, None, :])  96 us
    dynamic_update_slice x8, local copies, waits for them, and re-layouts, decode_blocks(): decoded = lax.map(decode_group, (packed_marker_groups, live_groups))  59.4 us
    convert_element_type x4, other arithmetic, decode_rows(): return centered.astype(jnp.bfloat16)  34.7 us
    dot_general x2, matrix products, per_device(): lax.dot_general(centered, solution_half, (((0,), (0,)), ((), ())), prefer...  26.3 us
    dot_general x2, matrix products, per_device(): jnp.dot(centered, snp_half, preferred_element_type=jnp.float32)  25.4 us
    dynamic_slice x12, local copies, waits for them, and re-layouts, decode_blocks(): decoded = lax.map(decode_group, (packed_marker_groups, live_groups))  20.5 us
    ppermute x6, starting transfers between devices, shifted(): return lax.ppermute(array, axis, pairs)  18 us
  transfers between devices with their start and end apart: 8, of which 2 were waited for; matrix products, arithmetic and copies ran while one was open for 52% of the time, Pallas kernels for 0%

commit v1 on v0

--- a/solution.py
+++ b/solution.py
@@ -128,7 +128,7 @@
         partial_sum = lax.dot_general(
             centered, solution_half, (((0,), (0,)), ((), ())), preferred_element_type=jnp.float32
         )
-        snp_half = lax.psum(partial_sum, "animal").astype(jnp.bfloat16)
+        snp_half = jnp.sum(lax.all_gather(partial_sum, "animal"), axis=0).astype(jnp.bfloat16)
         genomic_part = jnp.dot(centered, snp_half, preferred_element_type=jnp.float32)
         relatives = fetch_relatives(
             solution_half, relative_part, count_part, family_count, block_order, columns

time: 515 us -> 925 us (1.80)
  waiting for transfers between devices: 12.9 us -> 533 us
  blocking collectives: 184 us -> 15.8 us
  other arithmetic: 47 us -> 85.2 us
  between operations: 0.81 us -> 14.2 us
    all_gather x0 -> x2, waiting for transfers between devices: none -> 514 us  [per_device(): lax.all_gather(partial_sum, 'animal')]
    psum x2 -> x0, blocking collectives: 169 us -> none  [per_device(): snp_half = lax.psum(partial_sum, 'animal').astype(jnp.bfloat16)]
    reduce_sum x0 -> x2, other arithmetic: none -> 36.8 us  [per_device(): jnp.sum(lax.all_gather(partial_sum, 'animal'), axis=0).astype(jnp.bfloat16)]
  transfers between devices with their start and end apart: 8 -> 10, of which waited for: 2 -> 4; matrix products, arithmetic and copies ran while one was open for 52% -> 8% of each run, Pallas kernels for 0% -> 0%
where the time goes in v1:
time: 925 us; the launch traced here: 919 us
  waiting for transfers between devices  533 us (58%)
  local copies, waits for them, and re-layouts  182 us (20%)
  other arithmetic  85.2 us (9%)
  matrix products  54.7 us (6%)
  starting transfers between devices  34.4 us (4%)
  blocking collectives  15.8 us (2%)
  between operations  14.2 us (2%)
    all_gather x2, waiting for transfers between devices, per_device(): lax.all_gather(partial_sum, 'animal')  514 us
    shift_right_arithmetic x16, local copies, waits for them, and re-layouts, decode_rows(): jnp.right_shift(genotypes[:, :, None], bit_shifts[None, None, :])  96 us
    dynamic_update_slice x8, local copies, waits for them, and re-layouts, decode_blocks(): decoded = lax.map(decode_group, (packed_marker_groups, live_groups))  59.1 us
    reduce_sum x2, other arithmetic, per_device(): jnp.sum(lax.all_gather(partial_sum, 'animal'), axis=0).astype(jnp.bfloat16)  36.8 us
    convert_element_type x4, other arithmetic, decode_rows(): return centered.astype(jnp.bfloat16)  34.7 us
    dot_general x2, matrix products, per_device(): lax.dot_general(centered, solution_half, (((0,), (0,)), ((), ())), prefer...  26.5 us
    dot_general x2, matrix products, per_device(): jnp.dot(centered, snp_half, preferred_element_type=jnp.float32)  25.7 us
    ppermute x6, starting transfers between devices, shifted(): return lax.ppermute(array, axis, pairs)  23.1 us
  transfers between devices with their start and end apart: 10, of which 4 were waited for; matrix products, arithmetic and copies ran while one was open for 8% of the time, Pallas kernels for 0%

profile of v1, /device:TPU:0, one launch (start us, length us, event | category | flops | bytes accessed | tf_op | source)
XLA Modules:
  0.0 919.2 jit_solution(6162244264238367225)
XLA Ops:
  8.8 213.2 %while.10 = (s32[]{:T(128)}, bf16[4,512,6144]{2,1,0:T(8,128)(2,1)}, s32[4,512,1024]{2,1,0:T(8,128)}, f32[6144]{0:T(1024)}, f32[4,512]{1,0:T(4,128)S(1)}, /*index=5*/s32[]{:T(128)}) while((s32[]{:T(128)}, bf16[4,512,6144]{2,1,0:T(8,128)(2,1)}, s32[4,512,1024]{2,1,0:T(8,128)}, f32[6144]{0:T(1024)}, f32[4,512]{1,0:T(4,128)S(1)}, ...), condition=%wide.region_1.2_spmd, body=%wide.region_0.1_spmd.sunk | while | flops 18880520 | bytes 92453000 | solution.py:66
  23.1 15.6 %shift_right_arithmetic.40 = s32[1,512,6144]{1,2,0:T(8,128)} reshape(s32[512,1024,6]{0,2,1:T(8,128)} %shift_right_arithmetic.39) | data formatting | bytes 25165824 | tf_op jit(solution)/shard_map/while/body/eval_jaxpr/shift_right_arithmetic | solution.py:48
  38.7 8.7 multiply_convert_fusion.2
  47.4 8.7 copy.25
  76.4 15.6 %shift_right_arithmetic.40 = s32[1,512,6144]{1,2,0:T(8,128)} reshape(s32[512,1024,6]{0,2,1:T(8,128)} %shift_right_arithmetic.39) | data formatting | bytes 25165824 | tf_op jit(solution)/shard_map/while/body/eval_jaxpr/shift_right_arithmetic | solution.py:48
  92.0 8.7 multiply_convert_fusion.2
  100.7 8.7 copy.25
  129.7 15.6 %shift_right_arithmetic.40 = s32[1,512,6144]{1,2,0:T(8,128)} reshape(s32[512,1024,6]{0,2,1:T(8,128)} %shift_right_arithmetic.39) | data formatting | bytes 25165824 | tf_op jit(solution)/shard_map/while/body/eval_jaxpr/shift_right_arithmetic | solution.py:48
  145.3 8.7 multiply_convert_fusion.2
  154.0 8.7 copy.25
  183.0 15.6 %shift_right_arithmetic.40 = s32[1,512,6144]{1,2,0:T(8,128)} reshape(s32[512,1024,6]{0,2,1:T(8,128)} %shift_right_arithmetic.39) | data formatting | bytes 25165824 | tf_op jit(solution)/shard_map/while/body/eval_jaxpr/shift_right_arithmetic | solution.py:48
  198.6 8.7 multiply_convert_fusion.2
  223.5 13.3 %fusion.39 = f32[6144,128]{1,0:T(8,128)} fusion(bf16[2048,6144]{1,0:T(8,128)(2,1)} %bitcast.82, bf16[2048,128]{1,0:T(8,128)(2,1)S(1)} %get-tuple-element.51), kind=kOutput, calls=%fused_computation.72 | convolution fusion | flops 3221225472 | bytes 28835840 | tf_op jit(solution)/shard_map/dot_general | solution.py:128
  248.5 256.8 %all-gather.5.cloned.1.call-done = f32[98304,128]{1,0:T(8,128)} async-done(((f32[6144,128]{1,0:T(8,128)}), f32[98304,128]{1,0:T(8,128)}) %all-gather.5.cloned.1.call-update) | async-done | bytes 50331664 | tf_op jit(solution)/shard_map/all_gather | solution.py:131
  505.3 18.4 %reduce_sum.36 = bf16[6144,128]{1,0:T(8,128)(2,1)} reduce(f32[16,6144,128]{2,1,0:T(8,128)} %bitcast.64, f32[]{:T(128)} %constant.74.clone.1), dimensions={0}, to_apply=%region_2.3 | reduce | flops 11796480 | bytes 51904516 | tf_op jit(solution)/shard_map/reduce_sum | solution.py:131
  523.7 12.9 %fusion.2 = f32[8,256,128]{2,1,0:T(8,128)} fusion(bf16[8,256,6144]{2,1,0:T(8,128)(2,1)} %bitcast.83, bf16[6144,128]{1,0:T(8,128)(2,1)} %reduce_sum.36), kind=kOutput, calls=%fused_computation.12 | convolution fusion | flops 3221225472 | bytes 27787264 | tf_op jit(solution)/shard_map/dot_general | solution.py:132
  550.2 9.2 all-to-all-done
  560.6 15.8 %all_to_all.15 = bf16[8,256,128]{2,1,0:T(8,128)(2,1)S(1)} all-to-all(bf16[8,256,128]{2,1,0:T(8,128)(2,1)S(1)} %broadcast_in_dim.32), channel_id=1, replica_groups=mesh['animal'=16,'snp'=8] {'snp'}, dimensions={0} | all-to-all | bytes 1048576 | tf_op jit(solution)/shard_map/all_to_all | solution.py:31
  576.4 13.3 %fusion.40 = f32[6144,128]{1,0:T(8,128)} fusion(bf16[2048,6144]{1,0:T(8,128)(2,1)} %bitcast.84, bf16[2048,128]{1,0:T(8,128)(2,1)S(1)} %bitcast.67), kind=kOutput, calls=%fused_computation.73 | convolution fusion | flops 3221225472 | bytes 28835840 | tf_op jit(solution)/shard_map/dot_general | solution.py:128
  592.3 9.7 %collective-permute-start.5 = (bf16[2048,128]{1,0:T(8,128)(2,1)S(1)}, bf16[2048,128]{1,0:T(8,128)(2,1)}, u32[]{:S(2)}, u32[]{:S(2)}) collective-permute-start(bf16[2048,128]{1,0:T(8,128)(2,1)S(1)} %bitcast.70), channel_id=1, source_target_pairs={{0,24},{8,32},{16,40},{24,48},{32,56},{40,64},{48,72},{56,80},{64,... | collective-permute-start | bytes 1572872 | tf_op jit(solution)/shard_map/ppermute | solution.py:15
  602.0 257.4 %all-gather.7.cloned.1.call-done = f32[98304,128]{1,0:T(8,128)} async-done(((f32[6144,128]{1,0:T(8,128)}), f32[98304,128]{1,0:T(8,128)}) %all-gather.7.cloned.1.call-update) | async-done | bytes 50331664 | tf_op jit(solution)/shard_map/all_gather | solution.py:131
  859.4 18.4 %reduce_sum.38 = bf16[6144,128]{1,0:T(8,128)(2,1)} reduce(f32[16,6144,128]{2,1,0:T(8,128)} %bitcast.65, f32[]{:T(128)} %constant.74.clone.1), dimensions={0}, to_apply=%region_4.6 | reduce | flops 11796480 | bytes 51904516 | tf_op jit(solution)/shard_map/reduce_sum | solution.py:131
  877.8 12.9 %fusion = f32[8,256,128]{2,1,0:T(8,128)} fusion(bf16[8,256,6144]{2,1,0:T(8,128)(2,1)} %bitcast.85, bf16[6144,128]{1,0:T(8,128)(2,1)} %reduce_sum.38), kind=kOutput, calls=%fused_computation.10 | convolution fusion | flops 3221225472 | bytes 27787264 | tf_op jit(solution)/shard_map/dot_general | solution.py:132
  900.8 9.8 %all-to-all-done.2 = f32[8,256,128]{2,1,0:T(8,128)S(1)} async-done(((f32[8,256,128]{2,1,0:T(8,128)}), f32[8,256,128]{2,1,0:T(8,128)S(1)}, u32[]{:S(2)}, u32[]{:S(2)}) %all-to-all-start.2) | async-done | bytes 1048608 | tf_op jit(solution)/shard_map/all_to_all | solution.py:25
  (88 shorter events, 134.3 us)
Async XLA Ops:
  7.2 536.7 %copy-start = (bf16[16,128,128]{2,1,0:T(8,128)(2,1)S(1)}, bf16[16,128,128]{2,1,0:T(8,128)(2,1)}, u32[]{:S(2)}) copy-start(bf16[16,128,128]{2,1,0:T(8,128)(2,1)} %param.19) | copy-start | bytes 1572868
  7.2 498.2 %all-gather.5.cloned.1.call-start = ((), (), s32[]{:S(2)}) async-start(), calls=%async_computation.3 | async-start | bytes 53477376 | tf_op jit(solution)/shard_map/all_gather | solution.py:131
  223.4 24.9 %copy-start.2 = (s32[16]{0:T(128)S(1)}, s32[16]{0:T(128)}, u32[]{:S(2)}) copy-start(s32[16]{0:T(128)} %param.18) | copy-start | bytes 196
  223.4 25.0 %copy-start.1 = (s32[16]{0:T(128)S(1)}, s32[16]{0:T(128)}, u32[]{:S(2)}) copy-start(s32[16]{0:T(128)} %param.17) | copy-start | bytes 196
  236.8 307.2 %collective-permute-start.2 = (bf16[2048,128]{1,0:T(8,128)(2,1)S(1)}, bf16[2048,128]{1,0:T(8,128)(2,1)}, u32[]{:S(2)}, u32[]{:S(2)}) collective-permute-start(bf16[2048,128]{1,0:T(8,128)(2,1)S(1)} %get-tuple-element.51), channel_id=1, source_target_pairs={{0,24},{8,32},{16,40},{24,48},{32,56},{40,64},{48,72},{56,80},{64,... | collective-permute-start | bytes 1572872 | tf_op jit(solution)/shard_map/ppermute | solution.py:15
  240.5 303.5 %collective-permute-start.1 = (bf16[2048,128]{1,0:T(8,128)(2,1)S(1)}, bf16[2048,128]{1,0:T(8,128)(2,1)}, u32[]{:S(2)}, u32[]{:S(2)}) collective-permute-start(bf16[2048,128]{1,0:T(8,128)(2,1)S(1)} %get-tuple-element.51), channel_id=1, source_target_pairs={{0,16},{8,24},{16,32},{24,40},{32,48},{40,56},{48,64},{56,72},{64,... | collective-permute-start | bytes 1572872 | tf_op jit(solution)/shard_map/ppermute | solution.py:15
  245.1 298.9 %collective-permute-start = (bf16[2048,128]{1,0:T(8,128)(2,1)S(1)}, bf16[2048,128]{1,0:T(8,128)(2,1)}, u32[]{:S(2)}, u32[]{:S(2)}) collective-permute-start(bf16[2048,128]{1,0:T(8,128)(2,1)S(1)} %get-tuple-element.51), channel_id=1, source_target_pairs={{0,8},{8,16},{16,24},{24,32},{32,40},{40,48},{48,56},{56,64},{64,7... | collective-permute-start | bytes 1572872 | tf_op jit(solution)/shard_map/ppermute | solution.py:15
  536.6 22.8 %all-to-all-start = ((f32[8,256,128]{2,1,0:T(8,128)}), f32[8,256,128]{2,1,0:T(8,128)S(1)}, u32[]{:S(2)}, u32[]{:S(2)}) async-start(f32[8,256,128]{2,1,0:T(8,128)} %fusion.2), calls=%async_computation | async-start | bytes 2097152 | tf_op jit(solution)/shard_map/all_to_all | solution.py:25
  543.5 315.9 %all-gather.7.cloned.1.call-start = ((), (), s32[]{:S(2)}) async-start(), calls=%async_computation.4 | async-start | bytes 53477376 | tf_op jit(solution)/shard_map/all_gather | solution.py:131
  589.7 305.2 %collective-permute-start.4 = (bf16[2048,128]{1,0:T(8,128)(2,1)S(1)}, bf16[2048,128]{1,0:T(8,128)(2,1)S(1)}, u32[]{:S(2)}, u32[]{:S(2)}) collective-permute-start(bf16[2048,128]{1,0:T(8,128)(2,1)S(1)} %bitcast.68), channel_id=1, source_target_pairs={{0,16},{8,24},{16,32},{24,40},{32,48},{40,56},{48,64},{56,72},{64,... | collective-permute-start | bytes 1572872 | tf_op jit(solution)/shard_map/ppermute | solution.py:15
  591.0 303.9 %collective-permute-start.3 = (bf16[2048,128]{1,0:T(8,128)(2,1)S(1)}, bf16[2048,128]{1,0:T(8,128)(2,1)S(1)}, u32[]{:S(2)}, u32[]{:S(2)}) collective-permute-start(bf16[2048,128]{1,0:T(8,128)(2,1)S(1)} %bitcast.69), channel_id=1, source_target_pairs={{0,8},{8,16},{16,24},{24,32},{32,40},{40,48},{48,56},{56,64},{64,7... | collective-permute-start | bytes 1572872 | tf_op jit(solution)/shard_map/ppermute | solution.py:15
  592.3 302.6 %collective-permute-start.5 = (bf16[2048,128]{1,0:T(8,128)(2,1)S(1)}, bf16[2048,128]{1,0:T(8,128)(2,1)}, u32[]{:S(2)}, u32[]{:S(2)}) collective-permute-start(bf16[2048,128]{1,0:T(8,128)(2,1)S(1)} %bitcast.70), channel_id=1, source_target_pairs={{0,24},{8,32},{16,40},{24,48},{32,56},{40,64},{48,72},{56,80},{64,... | collective-permute-start | bytes 1572872 | tf_op jit(solution)/shard_map/ppermute | solution.py:15
  890.6 20.0 %all-to-all-start.2 = ((f32[8,256,128]{2,1,0:T(8,128)}), f32[8,256,128]{2,1,0:T(8,128)S(1)}, u32[]{:S(2)}, u32[]{:S(2)}) async-start(f32[8,256,128]{2,1,0:T(8,128)} %fusion), calls=%async_computation.2 | async-start | bytes 2097152 | tf_op jit(solution)/shard_map/all_to_all | solution.py:25
Sparse Core Ops, SparseCore 0:
  236.9 268.4 all-gather.4
  589.8 269.5 all-gather.6
